TPU v7x, 32 devices: a whole 2x2x4 slice. The times are simulated.
32 devices in a mesh: occ: 4 (over y, core), aux: 8 (over z, x).
Axes of the slice: x: 2, y: 2, z: 4, core: 2. Of those that a mesh axis runs over, the one named last changes fastest.
Arguments:
- pair_ints: bfloat16 [16, 128, 20480], P(None, None, ('aux', 'occ')), may hold values from -110 to 110
- domain_len: int32 [4], replicated, may hold values from 1 to 4, as said below
- domain_blocks: int32 [4, 4], replicated, may hold values from 0 to 703
- slot_orbital: int32 [4], replicated, may hold values from 0 to 3, each once
- virt_energy: float32 [90112], replicated, may hold values from 0.1 to 3
- occ_energy: float32 [4], replicated, may hold values from -2 to -0.3
Outputs:
- projected: bfloat16 [4, 512, 20480], P('occ', None, 'aux')
Inputs may be any that keep to these rules, and one draw needn't show every extreme that they name: `domain_len`: some orbital has exactly 4 live blocks. `slot_orbital`: each orbital is owned by exactly one group.
All inputs are finite; a program needn't handle non-finite values.
Results may differ from a plain program's by a relative error of at most 0.001.
The roundings to bfloat16 on the way count: a program that leaves them out, or rounds other values in their place, can miss the bound.
Values may be sent and summed in bfloat16 or wider, within the bound.
A program may use at most 128 MiB of HBM per device.

v0:
```python
import jax
import jax.numpy as jnp
from jax import lax
from jax.sharding import PartitionSpec as P

LEVEL_RATIO = 0.5
EPSILON = 1e-05


def local(pair_ints, domain_len, domain_blocks, slot_orbital, virt_energy, occ_energy):
    orbitals = domain_len.shape[0]
    block_count = domain_blocks.shape[1]
    block_rows = pair_ints.shape[1]
    local_cols = pair_ints.shape[2]
    domain_size = block_count * block_rows
    slot_ids = jnp.arange(block_count, dtype=jnp.int32)
    ordered_len = jnp.take(domain_len, slot_orbital, axis=0)
    starts = (slot_orbital * block_count)[:, None] + slot_ids[None, :]
    live_mask = slot_ids[None, :] < ordered_len[:, None]
    flat_index = starts.reshape(-1)
    picked = jnp.take(pair_ints, flat_index, axis=0)
    picked = jnp.where(live_mask.reshape(-1)[:, None, None], picked, jnp.zeros_like(picked))
    padded = picked.reshape(orbitals, domain_size, local_cols)
    regrouped = lax.all_to_all(padded, "occ", split_axis=0, concat_axis=2, tiled=True)
    own_rows = regrouped[0]
    owner_group = lax.axis_index("occ")
    orbital = lax.dynamic_index_in_dim(slot_orbital, owner_group, 0, keepdims=False)
    partials = jnp.einsum("oac,obc->oab", padded, padded, preferred_element_type=jnp.float32)
    gram_part = lax.psum_scatter(
        partials.reshape(orbitals * domain_size, domain_size),
        ("occ", "aux"),
        scatter_dimension=0,
        tiled=True,
    )
    gram_sum = lax.all_gather(gram_part, "aux", axis=0, tiled=True)
    energy_table = virt_energy.reshape(-1, block_rows)
    blocks = lax.dynamic_index_in_dim(domain_blocks, orbital, 0, keepdims=False)
    energies = jnp.take(energy_table, blocks, axis=0).reshape(domain_size)
    occ_level = lax.dynamic_index_in_dim(occ_energy, orbital, 0, keepdims=False)
    denominator = energies[:, None] + energies[None, :] - 2.0 * occ_level
    amplitude = gram_sum / denominator
    length = lax.dynamic_index_in_dim(domain_len, orbital, 0, keepdims=False).astype(jnp.float32)
    level_shift = LEVEL_RATIO * (jnp.trace(amplitude) / (block_rows * length) + EPSILON)
    factor = jnp.linalg.cholesky(amplitude + level_shift * jnp.eye(domain_size, dtype=jnp.float32))
    solved = jax.scipy.linalg.cho_solve((factor, True), amplitude)
    projector = solved.T.astype(jnp.bfloat16)
    projected = jnp.dot(projector, own_rows, preferred_element_type=jnp.float32).astype(
        jnp.bfloat16
    )
    return projected[None]


def solution(mesh):
    placed = (P(None, None, ("aux", "occ")), P(), P(), P(), P(), P())
    return jax.shard_map(
        local, mesh=mesh, in_specs=placed, out_specs=P("occ", None, "aux"), check_vma=False
    )
```

profile of v0, /device:TPU:0, one launch (start us, length us, event | category | flops | bytes accessed | tf_op | source)
XLA Modules:
  0.0 390.7 jit_solution(3105162862275415704)
XLA Ops:
  9.7 2.4 gather_fusion.1
  14.2 3.8 fusion.62
  18.1 4.7 %all-to-all-start = ((bf16[4,512,640]{2,1,0:T(8,128)(2,1)}), bf16[4,512,640]{2,1,0:T(8,128)(2,1)}, u32[]{:S(2)}, u32[]{:S(2)}) async-start(bf16[4,512,640]{2,1,0:T(8,128)(2,1)} %copy-done.2), calls=%async_computation | async-start | bytes 5242880 | tf_op jit(solution)/shard_map/all_to_all | solution.py:24
  22.8 143.1 %reduce-scatter.4.cloned.1.call-done = f32[64,512]{1,0:T(8,128)} async-done(((f32[2048,512]{1,0:T(8,128)}), f32[64,512]{1,0:T(8,128)}) %reduce-scatter.4.cloned.1.call-update) | async-done | bytes 131088 | tf_op jit(solution)/shard_map/reduce_scatter | solution.py:29
  173.1 4.8 %copy.58 = bf16[1,512,4,640]{1,3,2,0:T(8,128)(2,1)} copy(bf16[1,512,4,640]{3,1,2,0:T(8,128)(2,1)} %bitcast.23) | data formatting | bytes 5242880 | tf_op jit(solution)/shard_map/all_to_all | solution.py:24
  177.9 28.2 %all-gather.2.cloned.1.call-done = f32[512,512]{1,0:T(8,128)} async-done(((f32[64,512]{1,0:T(8,128)}), f32[512,512]{1,0:T(8,128)}) %all-gather.2.cloned.1.call-update) | async-done | bytes 1048592 | tf_op jit(solution)/shard_map/all_gather | solution.py:35
  206.2 2.6 copy.45
  208.8 3.2 select_reduce_fusion
  212.6 2.3 select_add_fusion
  215.0 2.5 copy.46
  220.3 11.7 %cholesky.103 = f32[128,128]{1,0:T(8,128)S(1)} custom-call(f32[128,128]{1,0:T(8,128)S(1)} %cholesky.263), custom_call_target="Cholesky" | custom-call | tf_op jit(solution)/shard_map/jit(cholesky)/cholesky | solution.py:44
  232.0 9.8 %custom-call.34 = f32[1,128,128]{1,2,0:T(8,128)S(1)} custom-call(f32[1,128,128]{2,1,0:T(8,128)S(1)} %get-tuple-element.46), custom_call_target="InvertDiagBlocksLowerTriangular" | custom-call | tf_op jit(solution)/shard_map/jit(cholesky)/cholesky | solution.py:44
  244.4 11.7 %cholesky.215 = f32[128,128]{1,0:T(8,128)S(1)} custom-call(f32[128,128]{1,0:T(8,128)S(1)} %cholesky.267), custom_call_target="Cholesky" | custom-call | tf_op jit(solution)/shard_map/jit(cholesky)/cholesky | solution.py:44
  256.5 10.0 %custom-call.35 = f32[1,128,128]{1,2,0:T(8,128)S(1)} custom-call(f32[1,128,128]{2,1,0:T(8,128)S(1)} %get-tuple-element.44), custom_call_target="InvertDiagBlocksLowerTriangular" | custom-call | tf_op jit(solution)/shard_map/jit(cholesky)/cholesky | solution.py:44
  269.4 11.7 %cholesky.236 = f32[128,128]{1,0:T(8,128)S(1)} custom-call(f32[128,128]{1,0:T(8,128)S(1)} %cholesky.272), custom_call_target="Cholesky" | custom-call | tf_op jit(solution)/shard_map/jit(cholesky)/cholesky | solution.py:44
  281.9 9.8 %custom-call.36 = f32[1,128,128]{1,2,0:T(8,128)S(1)} custom-call(f32[1,128,128]{2,1,0:T(8,128)S(1)} %get-tuple-element.42), custom_call_target="InvertDiagBlocksLowerTriangular" | custom-call | tf_op jit(solution)/shard_map/jit(cholesky)/cholesky | solution.py:44
  294.2 11.9 %cholesky.253 = f32[128,128]{1,0:T(8,128)S(1)} custom-call(f32[128,128]{1,0:T(8,128)S(1)} %convolution_subtract_fusion.8), custom_call_target="Cholesky" | custom-call | tf_op jit(solution)/shard_map/jit(cholesky)/cholesky | solution.py:44
  312.1 2.4 select_select_fusion
  314.5 14.2 %while.1 = (s32[]{:T(128)}, f32[512,512]{0,1:T(8,128)}, s32[4,2]{0,1:T(2,128)S(1)}, f32[4,128,128]{2,1,0:T(8,128)}, s32[]{:T(128)}) while((s32[]{:T(128)}, f32[512,512]{0,1:T(8,128)}, s32[4,2]{0,1:T(2,128)S(1)}, f32[4,128,128]{2,1,0:T(8,128)}, s32[]{:T(128)}) %tuple.32), condition=%wide.while_cond, body=%wide.while_body.sunk | while | flops 2 | bytes 393829 | solution.py:45
  315.1 2.2 dynamic-slice.7
  322.2 2.2 dynamic-slice.7
  328.7 40.1 %custom-call.37 = f32[4,128,128]{1,2,0:T(8,128)S(1)} custom-call(f32[4,128,128]{2,1,0:T(8,128)} %get-tuple-element.12), custom_call_target="InvertDiagBlocksLowerTriangular" | custom-call | tf_op jit(solution)/shard_map/jit(_cho_solve)/triangular_solve | solution.py:45
  374.8 2.4 convolution_subtract_fusion.5
  380.6 3.1 fusion
  (109 shorter events, 43.3 us)
Async XLA Ops:
  6.5 3.2 copy-start
  6.5 159.3 %reduce-scatter.4.cloned.1.call-start = ((), (), s32[]{:S(2)}) async-start(), calls=%async_computation.3 | async-start | bytes 4325376 | tf_op jit(solution)/shard_map/reduce_scatter | solution.py:29
  14.2 3.8 copy-start.2
  18.0 147.9 %copy-start.7 = (s32[4]{0:T(128)S(1)}, s32[4]{0:T(128)}, u32[]{:S(2)}) copy-start(s32[4]{0:T(128)} %param.9) | copy-start | bytes 52
  18.0 150.6 %copy-start.1 = (s32[4]{0:T(128)S(1)}, s32[4]{0:T(128)}, u32[]{:S(2)}) copy-start(s32[4]{0:T(128)} %param.7) | copy-start | bytes 52
  18.0 151.3 %copy-start.9 = (f32[4]{0:T(128)S(1)}, f32[4]{0:T(128)}, u32[]{:S(2)}) copy-start(f32[4]{0:T(128)} %param.11) | copy-start | bytes 52
  18.0 152.6 %copy-start.8 = (s32[4,4]{1,0:T(4,128)S(1)}, s32[4,4]{1,0:T(4,128)}, u32[]{:S(2)}) copy-start(s32[4,4]{1,0:T(4,128)} %param.8) | copy-start | bytes 196
  18.1 155.0 %all-to-all-start = ((bf16[4,512,640]{2,1,0:T(8,128)(2,1)}), bf16[4,512,640]{2,1,0:T(8,128)(2,1)}, u32[]{:S(2)}, u32[]{:S(2)}) async-start(bf16[4,512,640]{2,1,0:T(8,128)(2,1)} %copy-done.2), calls=%async_computation | async-start | bytes 5242880 | tf_op jit(solution)/shard_map/all_to_all | solution.py:24
  22.8 183.4 %all-gather.2.cloned.1.call-start = ((), (), s32[]{:S(2)}) async-start(), calls=%async_computation.2 | async-start | bytes 1179648 | tf_op jit(solution)/shard_map/all_gather | solution.py:35
  219.3 1.0 copy-start.5
  266.9 1.0 copy-start.3
  368.8 5.9 %copy-start.4 = (f32[512,512]{0,1:T(8,128)S(1)}, f32[512,512]{0,1:T(8,128)}, u32[]{:S(2)}) copy-start(f32[512,512]{0,1:T(8,128)} %get-tuple-element.107) | copy-start | bytes 3145732
  378.0 2.6 copy-start.6
Sparse Core Ops, SparseCore 0:
  18.1 147.6 reduce-scatter.3
  168.0 38.1 all-gather.1
where the time goes:
time: 394 us; the launch traced here: 391 us
  waiting for transfers between devices  171 us (43%)
  other arithmetic  133 us (34%)
  local copies, waits for them, and re-layouts  35.5 us (9%)
  matrix products  25.2 us (6%)
  between operations  20.8 us (5%)
  starting transfers between devices  4.74 us (1%)
    reduce_scatter x1, waiting for transfers between devices, local(): lax.psum_scatter(partials.reshape(orbitals * domain_size, domain_size), (...  143 us
    another operation x15, other arithmetic, local(): jnp.linalg.cholesky(amplitude + level_shift * jnp.eye(domain_size, dtype=...  79.4 us
    another operation x3, other arithmetic, local(): solved = jax.scipy.linalg.cho_solve((factor, True), amplitude)  42.5 us
    all_gather x1, waiting for transfers between devices, local(): gram_sum = lax.all_gather(gram_part, 'aux', axis=0, tiled=True)  28.2 us
    another operation x20, local copies, waits for them, and re-layouts  14.2 us
    another operation x14, matrix products, local(): solved = jax.scipy.linalg.cho_solve((factor, True), amplitude)  11.6 us
  transfers between devices with their start and end apart: 3, of which 2 were waited for; matrix products, arithmetic and copies ran while one was open for 2% of the time, Pallas kernels for 0%

commit v1 on v0

--- a/solution.py
+++ b/solution.py
@@ -5,6 +5,29 @@
 
 LEVEL_RATIO = 0.5
 EPSILON = 1e-05
+
+
+def list_the_rails(mine_x, ndim_at):
+    heard = list(mine_x.shape[1:])
+    heard[ndim_at] *= mine_x.shape[0]
+    return jnp.moveaxis(mine_x, 0, ndim_at).reshape(heard)
+
+
+def begin_the_samples(inputs, link_axis):
+    found_now = inputs[None]
+    axis_len = lax.axis_size(link_axis)
+    for num in range(axis_len.bit_length() - 1):
+        val2 = 1 << num
+        rows = []
+        k0 = 0
+        while k0 < axis_len:
+            rows.append((k0, k0 ^ val2))
+            k0 += 1
+        part_now = lax.ppermute(found_now, link_axis, rows)
+        y_new = jnp.stack([found_now, part_now], axis=0)
+        reached = lax.axis_index(link_axis) >> num & 1
+        found_now = jnp.where(reached == 0, y_new, y_new[::-1]).reshape(-1, *inputs.shape)
+    return found_now
 
 
 def local(pair_ints, domain_len, domain_blocks, slot_orbital, virt_energy, occ_energy):
@@ -32,7 +55,7 @@
         scatter_dimension=0,
         tiled=True,
     )
-    gram_sum = lax.all_gather(gram_part, "aux", axis=0, tiled=True)
+    gram_sum = list_the_rails(begin_the_samples(gram_part, "aux"), 0)
     energy_table = virt_energy.reshape(-1, block_rows)
     blocks = lax.dynamic_index_in_dim(domain_blocks, orbital, 0, keepdims=False)
     energies = jnp.take(energy_table, blocks, axis=0).reshape(domain_size)

time: 394 us -> 390 us (0.990)
  waiting for transfers between devices: 171 us -> 164 us
    all_gather x1 -> x0, waiting for transfers between devices: 28.2 us -> none  [local(): gram_sum = lax.all_gather(gram_part, 'aux', axis=0, tiled=True)]
    ppermute x0 -> x3, waiting for transfers between devices: none -> 23.7 us  [begin_the_samples(): part_now = lax.ppermute(found_now, link_axis, rows)]
    another operation x20 -> x21, local copies, waits for them, and re-layouts: 14.2 us -> 16.8 us
  transfers between devices with their start and end apart: 3 -> 5, of which waited for: 2 -> 4; matrix products, arithmetic and copies ran while one was open for 2% -> 3% of each run, Pallas kernels for 0% -> 0%
where the time goes in v1:
time: 390 us; the launch traced here: 385 us
  waiting for transfers between devices  164 us (42%)
  other arithmetic  135 us (35%)
  local copies, waits for them, and re-layouts  36 us (9%)
  matrix products  25.2 us (6%)
  between operations  20.4 us (5%)
  starting transfers between devices  4.84 us (1%)
    reduce_scatter x1, waiting for transfers between devices, local(): lax.psum_scatter(partials.reshape(orbitals * domain_size, domain_size), (...  141 us
    another operation x15, other arithmetic, local(): jnp.linalg.cholesky(amplitude + level_shift * jnp.eye(domain_size, dtype=...  79.3 us
    another operation x3, other arithmetic, local(): solved = jax.scipy.linalg.cho_solve((factor, True), amplitude)  42.5 us
    ppermute x3, waiting for transfers between devices, begin_the_samples(): part_now = lax.ppermute(found_now, link_axis, rows)  23.7 us
    another operation x20, local copies, waits for them, and re-layouts  14.2 us
    another operation x14, matrix products, local(): solved = jax.scipy.linalg.cho_solve((factor, True), amplitude)  11.6 us
  transfers between devices with their start and end apart: 5, of which 4 were waited for; matrix products, arithmetic and copies ran while one was open for 3% of the time, Pallas kernels for 0%

profile of v1, /device:TPU:0, one launch (start us, length us, event | category | flops | bytes accessed | tf_op | source)
XLA Modules:
  0.0 385.5 jit_solution(2978926060407947458)
XLA Ops:
  9.7 2.4 gather_fusion.1
  14.2 3.8 fusion.65
  18.1 4.7 %all-to-all-start = ((bf16[4,512,640]{2,1,0:T(8,128)(2,1)}), bf16[4,512,640]{2,1,0:T(8,128)(2,1)}, u32[]{:S(2)}, u32[]{:S(2)}) async-start(bf16[4,512,640]{2,1,0:T(8,128)(2,1)} %copy-done.2), calls=%async_computation.1 | async-start | bytes 5242880 | tf_op jit(solution)/shard_map/all_to_all | solution.py:47
  25.3 140.7 %reduce-scatter.2.cloned.1.call-done = f32[64,512]{1,0:T(8,128)} async-done(((f32[2048,512]{1,0:T(8,128)}), f32[64,512]{1,0:T(8,128)}) %reduce-scatter.2.cloned.1.call-update) | async-done | bytes 131088 | tf_op jit(solution)/shard_map/reduce_scatter | solution.py:52
  166.1 5.1 %collective-permute-done = f32[1,64,512]{2,1,0:T(8,128)S(1)} collective-permute-done((f32[1,64,512]{2,1,0:T(8,128)}, f32[1,64,512]{2,1,0:T(8,128)S(1)}, u32[]{:S(2)}, u32[]{:S(2)}) %collective-permute-start) | collective-permute-done | bytes 131104 | tf_op jit(solution)/shard_map/ppermute | solution.py:26
  176.8 3.6 collective-permute-done.1
  180.7 4.8 %copy.43 = bf16[1,512,4,640]{1,3,2,0:T(8,128)(2,1)} copy(bf16[1,512,4,640]{3,1,2,0:T(8,128)(2,1)} %bitcast.33) | data formatting | bytes 5242880 | tf_op jit(solution)/shard_map/all_to_all | solution.py:47
  185.5 15.0 %collective-permute-done.2 = f32[4,64,512]{2,1,0:T(8,128)} collective-permute-done((f32[4,64,512]{2,1,0:T(8,128)S(1)}, f32[4,64,512]{2,1,0:T(8,128)}, u32[]{:S(2)}, u32[]{:S(2)}) %collective-permute-start.2) | collective-permute-done | bytes 524320 | tf_op jit(solution)/shard_map/ppermute | solution.py:26
  203.6 2.6 copy.30
  206.8 2.8 select_add_fusion
  209.6 2.5 copy.31
  215.0 11.7 %cholesky.103 = f32[128,128]{1,0:T(8,128)S(1)} custom-call(f32[128,128]{1,0:T(8,128)S(1)} %cholesky.263), custom_call_target="Cholesky" | custom-call | tf_op jit(solution)/shard_map/jit(cholesky)/cholesky | solution.py:67
  226.7 9.8 %custom-call.34 = f32[1,128,128]{1,2,0:T(8,128)S(1)} custom-call(f32[1,128,128]{2,1,0:T(8,128)S(1)} %get-tuple-element.46), custom_call_target="InvertDiagBlocksLowerTriangular" | custom-call | tf_op jit(solution)/shard_map/jit(cholesky)/cholesky | solution.py:67
  239.0 11.7 %cholesky.215 = f32[128,128]{1,0:T(8,128)S(1)} custom-call(f32[128,128]{1,0:T(8,128)S(1)} %cholesky.267), custom_call_target="Cholesky" | custom-call | tf_op jit(solution)/shard_map/jit(cholesky)/cholesky | solution.py:67
  251.3 9.8 %custom-call.35 = f32[1,128,128]{1,2,0:T(8,128)S(1)} custom-call(f32[1,128,128]{2,1,0:T(8,128)S(1)} %get-tuple-element.44), custom_call_target="InvertDiagBlocksLowerTriangular" | custom-call | tf_op jit(solution)/shard_map/jit(cholesky)/cholesky | solution.py:67
  264.1 11.7 %cholesky.236 = f32[128,128]{1,0:T(8,128)S(1)} custom-call(f32[128,128]{1,0:T(8,128)S(1)} %cholesky.272), custom_call_target="Cholesky" | custom-call | tf_op jit(solution)/shard_map/jit(cholesky)/cholesky | solution.py:67
  276.6 9.8 %custom-call.36 = f32[1,128,128]{1,2,0:T(8,128)S(1)} custom-call(f32[1,128,128]{2,1,0:T(8,128)S(1)} %get-tuple-element.42), custom_call_target="InvertDiagBlocksLowerTriangular" | custom-call | tf_op jit(solution)/shard_map/jit(cholesky)/cholesky | solution.py:67
  288.9 11.9 %cholesky.253 = f32[128,128]{1,0:T(8,128)S(1)} custom-call(f32[128,128]{1,0:T(8,128)S(1)} %convolution_subtract_fusion.8), custom_call_target="Cholesky" | custom-call | tf_op jit(solution)/shard_map/jit(cholesky)/cholesky | solution.py:67
  306.8 2.4 select_select_fusion
  309.2 14.2 %while.1 = (s32[]{:T(128)}, f32[512,512]{0,1:T(8,128)}, s32[4,2]{0,1:T(2,128)S(1)}, f32[4,128,128]{2,1,0:T(8,128)}, s32[]{:T(128)}) while((s32[]{:T(128)}, f32[512,512]{0,1:T(8,128)}, s32[4,2]{0,1:T(2,128)S(1)}, f32[4,128,128]{2,1,0:T(8,128)}, s32[]{:T(128)}) %tuple.33), condition=%wide.while_cond, body=%wide.while_body.sunk | while | flops 2 | bytes 393829 | solution.py:68
  313.4 2.2 dynamic-slice.7
  323.4 40.1 %custom-call.37 = f32[4,128,128]{1,2,0:T(8,128)S(1)} custom-call(f32[4,128,128]{2,1,0:T(8,128)} %get-tuple-element.12), custom_call_target="InvertDiagBlocksLowerTriangular" | custom-call | tf_op jit(solution)/shard_map/jit(_cho_solve)/triangular_solve | solution.py:68
  369.5 2.4 convolution_subtract_fusion.5
  375.3 3.1 fusion
  (125 shorter events, 50.4 us)
Async XLA Ops:
  6.5 3.2 copy-start
  6.5 159.5 %reduce-scatter.2.cloned.1.call-start = ((), (), s32[]{:S(2)}) async-start(), calls=%async_computation.2 | async-start | bytes 4325376 | tf_op jit(solution)/shard_map/reduce_scatter | solution.py:52
  14.2 3.8 copy-start.2
  18.0 4.8 %copy-start.7 = (s32[4]{0:T(128)S(1)}, s32[4]{0:T(128)}, u32[]{:S(2)}) copy-start(s32[4]{0:T(128)} %param.9) | copy-start | bytes 52
  18.0 7.2 %copy-start.8 = (s32[4,4]{1,0:T(4,128)S(1)}, s32[4,4]{1,0:T(4,128)}, u32[]{:S(2)}) copy-start(s32[4,4]{1,0:T(4,128)} %param.8) | copy-start | bytes 196
  18.0 154.3 %copy-start.1 = (s32[4]{0:T(128)S(1)}, s32[4]{0:T(128)}, u32[]{:S(2)}) copy-start(s32[4]{0:T(128)} %param.7) | copy-start | bytes 52
  18.0 156.8 %copy-start.9 = (f32[4]{0:T(128)S(1)}, f32[4]{0:T(128)}, u32[]{:S(2)}) copy-start(f32[4]{0:T(128)} %param.11) | copy-start | bytes 52
  18.1 162.6 %all-to-all-start = ((bf16[4,512,640]{2,1,0:T(8,128)(2,1)}), bf16[4,512,640]{2,1,0:T(8,128)(2,1)}, u32[]{:S(2)}, u32[]{:S(2)}) async-start(bf16[4,512,640]{2,1,0:T(8,128)(2,1)} %copy-done.2), calls=%async_computation.1 | async-start | bytes 5242880 | tf_op jit(solution)/shard_map/all_to_all | solution.py:47
  166.1 5.2 %collective-permute-start = (f32[1,64,512]{2,1,0:T(8,128)}, f32[1,64,512]{2,1,0:T(8,128)S(1)}, u32[]{:S(2)}, u32[]{:S(2)}) collective-permute-start(f32[1,64,512]{2,1,0:T(8,128)} %bitcast.119), channel_id=1, source_target_pairs={{0,1},{1,0},{2,3},{3,2},{4,5},{5,4},{6,7},{7,6},{8,9},{9,8},{10,11... | collective-permute-start | bytes 393224 | tf_op jit(solution)/shard_map/ppermute | solution.py:26
  172.3 8.1 %collective-permute-start.1 = (f32[2,64,512]{2,1,0:T(8,128)S(1)}, f32[2,64,512]{2,1,0:T(8,128)S(1)}, u32[]{:S(2)}, u32[]{:S(2)}) collective-permute-start(f32[2,64,512]{2,1,0:T(8,128)S(1)} %get-tuple-element.40), channel_id=1, source_target_pairs={{0,2},{1,3},{2,0},{3,1},{4,6},{5,7},{6,4},{7,5},{8,10},{9,11},{10,... | collective-permute-start | bytes 786440 | tf_op jit(solution)/shard_map/ppermute | solution.py:26
  180.5 20.0 %collective-permute-start.2 = (f32[4,64,512]{2,1,0:T(8,128)S(1)}, f32[4,64,512]{2,1,0:T(8,128)}, u32[]{:S(2)}, u32[]{:S(2)}) collective-permute-start(f32[4,64,512]{2,1,0:T(8,128)S(1)} %bitcast.116), channel_id=1, source_target_pairs={{0,4},{1,5},{2,6},{3,7},{4,0},{5,1},{6,2},{7,3},{8,12},{9,13},{10,... | collective-permute-start | bytes 1572872 | tf_op jit(solution)/shard_map/ppermute | solution.py:26
  213.9 1.0 copy-start.5
  261.6 1.0 copy-start.3
  363.6 5.9 %copy-start.4 = (f32[512,512]{0,1:T(8,128)S(1)}, f32[512,512]{0,1:T(8,128)}, u32[]{:S(2)}) copy-start(f32[512,512]{0,1:T(8,128)} %get-tuple-element.106) | copy-start | bytes 3145732
  372.7 2.6 copy-start.6
Sparse Core Ops, SparseCore 0:
  18.1 147.9 reduce-scatter.1
